TPU v7x, 32 devices: a whole 2x2x4 slice. The times are simulated.
32 devices in a mesh: grp: 2 (over y), smp: 4 (over z), blk: 2 (over x), pen: 2 (over core).
Axes of the slice: x: 2, y: 2, z: 4, core: 2. Of those that a mesh axis runs over, the one named last changes fastest.
Arguments:
- allele_matrix: bfloat16 [2048, 4096], P('smp', ('grp', 'blk')), parts along dimension 1, may hold values from -6 to 6
- orthonormal_frames: bfloat16 [8, 512, 512], P(('grp', 'blk')), parts along dimension 0, may hold values from -0.25 to 0.25
- segment_variances: float32 [8, 512], P(('grp', 'blk')), parts along dimension 0, may hold values from 20.48 to 2048
- lambda_grid: float32 [4], replicated, may hold values from 20.48 to 2048
- trait_levels: bfloat16 [2048, 256], P('smp', ('grp', 'pen')), parts along dimension 1, may hold values from -6 to 6
- partition_labels: int32 [2048], P('smp'), may hold values from 0 to 3
- preceding_fits: bfloat16 [4, 2048, 1536], P(('grp', 'pen'), 'smp', 'blk'), parts along dimension 0, may hold values from -6 to 6
Outputs:
- level0_predictions: bfloat16 [2048, 8, 4, 128], P('smp', ('grp', 'blk'), None, 'pen'), parts along dimension 1
- gram_old: float32 [4, 1536, 1536], P(('grp', 'pen'), 'blk', 'smp'), parts along dimension 0
- gram_cross: float32 [4, 16, 1536], P(('grp', 'pen'), 'blk', 'smp'), parts along dimension 0
- gram_new: float32 [4, 16, 16], P(('grp', 'pen'), 'blk'), parts along dimension 0
- fit_old: float32 [4, 1536], P(('grp', 'pen'), 'smp'), parts along dimension 0
- fit_new: float32 [4, 16], P(('grp', 'pen'), 'blk'), parts along dimension 0
There are 2 independent parts, one for each index of `grp`. A program takes and returns all parts, laid end to end along the dimension named above; an argument that names none is the same for every part. Nothing has to cross between parts.
All inputs are finite; a program needn't handle non-finite values.
Results may differ from a plain program's by a relative error of at most 0.018.
Values may be sent and summed in bfloat16 or wider, within the bound.
A program may use at most 64 MiB of HBM per device.

v0:
```python
import jax
import jax.numpy as jnp
from jax import lax
from jax.sharding import PartitionSpec as P

FOLDS = 4


def segment_fitted_trait(
    projected_traits, pairwise_inner, spectral_line, lambda_grid, partition_mask_real
):
    var_width = projected_traits.shape[1]
    prot_width = pairwise_inner.shape[1] // FOLDS
    lambda_grid_size = lambda_grid.shape[0]
    pairwise_inner = pairwise_inner.reshape(var_width, FOLDS, prot_width)
    remainder = jnp.sum(pairwise_inner, axis=1, keepdims=True) - pairwise_inner
    damping_ratio = 1.0 / (spectral_line[:, None] + lambda_grid[None, :])
    ridge_coefficients = (remainder[:, :, None, :] * damping_ratio[:, None, :, None]).astype(
        jnp.bfloat16
    )
    row_count = projected_traits.shape[0]
    running_total = jnp.zeros((row_count, lambda_grid_size * prot_width), jnp.float32)
    for holdout_index in range(FOLDS):
        lookup_table = ridge_coefficients[:, holdout_index].reshape(
            var_width, lambda_grid_size * prot_width
        )
        running_total = running_total + partition_mask_real[
            :, holdout_index : holdout_index + 1
        ] * jnp.dot(projected_traits, lookup_table, preferred_element_type=jnp.float32)
    return running_total.reshape(row_count, lambda_grid_size, prot_width).astype(jnp.bfloat16)


def sum_block(local_cross):
    return lax.psum(local_cross, "smp")


def per_device(
    allele_matrix,
    orthonormal_frames,
    segment_variances,
    lambda_grid,
    trait_levels,
    partition_labels,
    preceding_fits,
):
    row_count = allele_matrix.shape[0]
    block_count = orthonormal_frames.shape[0]
    var_width = orthonormal_frames.shape[1]
    prot_width = trait_levels.shape[1]
    lambda_grid_size = lambda_grid.shape[0]
    sample_total = float(row_count * lax.axis_size("smp"))
    contract = (((0,), (0,)), ((), ()))
    member = partition_labels[:, None] == jnp.arange(FOLDS, dtype=jnp.int32)[None, :]
    partition_mask_real = member.astype(jnp.float32)
    masked = (member.astype(jnp.bfloat16)[:, :, None] * trait_levels[:, None, :]).reshape(
        row_count, FOLDS * prot_width
    )
    rotated_list = []
    local_list = []
    for entry_offset in range(block_count):
        genotype_cols = allele_matrix[:, entry_offset * var_width : (entry_offset + 1) * var_width]
        projected_traits = jnp.dot(
            genotype_cols, orthonormal_frames[entry_offset], preferred_element_type=jnp.float32
        ).astype(jnp.bfloat16)
        rotated_list.append(projected_traits)
        local_list.append(
            lax.dot_general(projected_traits, masked, contract, preferred_element_type=jnp.float32)
        )
    crossed_list = [sum_block(local_cross) for local_cross in local_list]
    pred_list = [
        segment_fitted_trait(
            rotated_list[entry_offset],
            crossed_list[entry_offset],
            segment_variances[entry_offset],
            lambda_grid,
            partition_mask_real,
        )
        for entry_offset in range(block_count)
    ]
    level0_predictions = jnp.stack(pred_list, axis=1)
    added_columns = level0_predictions[:, :, :, 0].reshape(
        row_count, block_count * lambda_grid_size
    )
    target = trait_levels[:, 0:1]
    old_cols = preceding_fits[0]
    old_width = old_cols.shape[1]
    new_width = added_columns.shape[1]
    joined = jnp.concatenate([old_cols, added_columns], axis=1)
    gathered = lax.all_gather(joined, "blk", axis=1, tiled=True)
    shard_count = gathered.shape[1] // joined.shape[1]
    pieces = gathered.reshape(row_count, shard_count, joined.shape[1])
    old_all = pieces[:, :, :old_width].reshape(row_count, shard_count * old_width)
    new_all = pieces[:, :, old_width:].reshape(row_count, shard_count * new_width)
    stacked = jnp.concatenate([old_cols, added_columns, target], axis=1)
    reduced = lax.psum_scatter(
        lax.dot_general(stacked, old_all, contract, preferred_element_type=jnp.float32),
        "smp",
        scatter_dimension=1,
        tiled=True,
    )
    gram_old = reduced[:old_width]
    gram_cross = reduced[old_width : old_width + new_width]
    fit_old = reduced[old_width + new_width :]
    right_side = jnp.concatenate([new_all, target], axis=1)
    small_gram = lax.psum(
        lax.dot_general(added_columns, right_side, contract, preferred_element_type=jnp.float32),
        "smp",
    )
    gram_new = small_gram[:, :-1]
    fit_new = small_gram[:, -1]
    return (
        level0_predictions,
        (gram_old / sample_total)[None],
        (gram_cross / sample_total)[None],
        (gram_new / sample_total)[None],
        fit_old / sample_total,
        (fit_new / sample_total)[None],
    )


def solution(mesh):
    placed = (
        P("smp", ("grp", "blk")),
        P(("grp", "blk"), None, None),
        P(("grp", "blk"), None),
        P(),
        P("smp", ("grp", "pen")),
        P("smp"),
        P(("grp", "pen"), "smp", "blk"),
    )
    return jax.shard_map(
        per_device,
        mesh=mesh,
        in_specs=placed,
        out_specs=(
            P("smp", ("grp", "blk"), None, "pen"),
            P(("grp", "pen"), "blk", "smp"),
            P(("grp", "pen"), "blk", "smp"),
            P(("grp", "pen"), "blk", None),
            P(("grp", "pen"), "smp"),
            P(("grp", "pen"), "blk"),
        ),
        check_vma=False,
    )
```

profile of v0, /device:TPU:0, one launch (start us, length us, event | category | flops | bytes accessed | tf_op | source)
XLA Modules:
  0.0 205.0 jit_solution(1998468806075060013)
XLA Ops:
  7.2 1.7 convolution_convert_fusion
  9.0 1.5 convolution_convert_fusion.1
  10.5 1.1 fusion.36
  11.6 1.1 fusion.37
  12.8 0.3 copy.19
  13.1 0.3 copy-done.3
  13.5 54.1 %all-reduce.3.cloned.1.call-done = (f32[512,4,64]{0,2,1:T(8,128)}, f32[512,4,64]{0,2,1:T(8,128)}) async-done(((f32[512,4,64]{0,2,1:T(8,128)}, f32[512,4,64]{0,2,1:T(8,128)}), (f32[512,4,64]{0,2,1:T(8,128)}, f32[512,4,64]{0,2,1:T(8,128)})) %all-reduce.3.cloned.1.call-update) | async-done | bytes 1048592 | tf_op jit(solution)/shard_map/psum | solution.py:34
  67.6 1.1 reduce_sum.19
  68.7 1.1 broadcast_subtract_fusion
  70.0 0.5 multiply_convert_fusion
  70.7 0.3 convolution_multiply_fusion.3
  71.0 0.3 convolution_multiply_fusion.7
  71.3 0.3 fusion.2
  71.7 0.3 fusion.5
  72.0 0.3 fusion.1
  72.4 0.3 fusion.4
  72.7 0.3 fusion.7
  73.1 0.3 fusion.6
  73.5 0.9 pad_maximum_fusion
  74.5 26.7 %all-gather.2.cloned.1.call-done = bf16[512,1552]{0,1:T(8,128)(2,1)} async-done(((bf16[512,776]{0,1:T(8,128)(2,1)}), bf16[512,1552]{0,1:T(8,128)(2,1)}) %all-gather.2.cloned.1.call-update) | async-done | bytes 1589264 | tf_op jit(solution)/shard_map/all_gather | solution.py:89
  101.2 1.5 slice.126
  102.7 3.6 %fusion.9 = f32[777,1536]{1,0:T(8,128)} fusion(bf16[512,1536]{0,1:T(8,128)(2,1)S(1)} %bitcast.73, bf16[512,1]{0,1:T(2,128)(2,1)S(1)} %slice.104, bf16[512,8]{0,1:T(8,128)(2,1)S(1)} %reshape_squeeze.35, bf16[512,768]{0,1:T(8,128)(2,1)S(1)} %bitcast.62), kind=kOutput, calls=%fused_computation.22 | convolution fusion | flops 1224502272 | bytes 7142400 | tf_op jit(solution)/shard_map/dot_general | solution.py:96
  106.3 0.8 pad_maximum_fusion.1
  107.2 0.7 slice_bitcast_fusion
  107.9 0.1 fusion.21
  108.0 12.1 %psum.23 = f32[8,17]{1,0:T(8,128)S(1)} all-reduce(f32[8,17]{1,0:T(8,128)S(1)} %fusion.21), channel_id=1, replica_groups=mesh['grp'=2,'smp'=4,'blk'=2,'pen'=2] {'smp'}, use_global_device_ids=true, to_apply=%region_5.0 | all-reduce | flops 136 | bytes 1088 | tf_op jit(solution)/shard_map/psum | solution.py:105
  120.1 0.7 multiply_reduce_fusion
  120.8 0.6 multiply_bitcast_fusion
  121.4 72.1 %reduce-scatter.2.cloned.1.call-done = f32[777,384]{1,0:T(8,128)} async-done(((f32[777,1536]{1,0:T(8,128)}), f32[777,384]{1,0:T(8,128)}) %reduce-scatter.2.cloned.1.call-update) | async-done | bytes 1193488 | tf_op jit(solution)/shard_map/reduce_scatter | solution.py:95
  193.5 1.3 slice_multiply_fusion.2
  194.8 1.3 fusion.27
  196.1 2.4 %fusion.8 = f32[1,768,384]{2,1,0:T(8,128)} fusion(f32[777,384]{1,0:T(8,128)} %reduce-scatter.2.cloned.1.call-done), kind=kLoop, calls=%fused_computation.21 | loop fusion | flops 294912 | bytes 2359296 | tf_op jit(solution)/shard_map/broadcast_in_dim | solution.py:113
  (31 shorter events, 0.6 us)
Async XLA Ops:
  7.2 3.3 %copy-start.4 = (s32[512]{0:T(512)S(1)}, s32[512]{0:T(512)}, u32[]{:S(2)}) copy-start(s32[512]{0:T(512)} %param.12) | copy-start | bytes 6148
  7.2 3.3 %copy-start.2 = (bf16[512,64]{0,1:T(8,128)(2,1)S(1)}, bf16[512,64]{0,1:T(8,128)(2,1)}, u32[]{:S(2)}) copy-start(bf16[512,64]{0,1:T(8,128)(2,1)} %param.11) | copy-start | bytes 196612
  7.2 60.4 %all-reduce.3.cloned.1.call-start = ((), (), s32[]{:S(2)}) async-start(), calls=%async_computation.3 | async-start | bytes 2097152 | tf_op jit(solution)/shard_map/psum | solution.py:34
  7.2 1.7 copy-start.6
  10.5 2.3 %copy-start.1 = (bf16[1,512,768]{2,1,0:T(8,128)(2,1)S(1)}, bf16[1,512,768]{2,1,0:T(8,128)(2,1)}, u32[]{:S(2)}) copy-start(bf16[1,512,768]{2,1,0:T(8,128)(2,1)} %param.13) | copy-start | bytes 2359300
  12.7 0.7 copy-start.3
  12.7 0.7 copy-start.5
  12.8 88.4 %all-gather.2.cloned.1.call-start = ((), (), s32[]{:S(2)}) async-start(), calls=%async_computation.1 | async-start | bytes 2383872 | tf_op jit(solution)/shard_map/all_gather | solution.py:89
  67.6 2.3 %copy-start = (f32[512,4,64]{0,2,1:T(8,128)S(1)}, f32[512,4,64]{0,2,1:T(8,128)}, u32[]{:S(2)}) copy-start(f32[512,4,64]{0,2,1:T(8,128)} %get-tuple-element.7) | copy-start | bytes 1572868
  74.4 119.1 %reduce-scatter.2.cloned.1.call-start = ((), (), s32[]{:S(2)}) async-start(), calls=%async_computation.2 | async-start | bytes 6021120 | tf_op jit(solution)/shard_map/reduce_scatter | solution.py:95
Sparse Core Ops, SparseCore 0:
  12.9 54.6 all-reduce.2
  74.5 26.5 all-gather.1
  106.4 87.0 reduce-scatter.1
where the time goes:
time: 205 us
  waiting for transfers between devices  153 us (75%)
  between operations  14 us (7%)
  blocking collectives  12.1 us (6%)
  matrix products  11.8 us (6%)
  other arithmetic  11 us (5%)
  local copies, waits for them, and re-layouts  3.02 us (1%)
    reduce_scatter x1, waiting for transfers between devices, per_device(): lax.psum_scatter(lax.dot_general(stacked, old_all, contract, preferred_el...  72.1 us
    psum x1, waiting for transfers between devices, sum_block(): return lax.psum(local_cross, 'smp')  54.1 us
    all_gather x1, waiting for transfers between devices, per_device(): gathered = lax.all_gather(joined, 'blk', axis=1, tiled=True)  26.7 us
    psum x1, blocking collectives, per_device(): lax.psum(lax.dot_general(added_columns, right_side, contract, preferred_e...  12.1 us
  transfers between devices with their start and end apart: 3, of which 3 were waited for; matrix products, arithmetic and copies ran while one was open for 2% of the time, Pallas kernels for 0%

commit v1 on v0

--- a/solution.py
+++ b/solution.py
@@ -4,6 +4,12 @@
 from jax.sharding import PartitionSpec as P
 
 FOLDS = 4
+
+
+def gather_and_add(x, mesh_axis):
+    terms = lax.all_gather(x, mesh_axis, axis=0, tiled=False)
+    total = terms.sum(axis=0)
+    return total
 
 
 def segment_fitted_trait(
@@ -31,7 +37,7 @@
 
 
 def sum_block(local_cross):
-    return lax.psum(local_cross, "smp")
+    return gather_and_add(local_cross, "smp")
 
 
 def per_device(

time: 205 us -> 244 us (1.19)
  waiting for transfers between devices: 153 us -> 187 us
  other arithmetic: 11 us -> 14 us
    all_gather x0 -> x2, waiting for transfers between devices: none -> 89.6 us  [gather_and_add(): terms = lax.all_gather(x, mesh_axis, axis=0, tiled=False)]
    psum x1 -> x0, waiting for transfers between devices: 54.1 us -> none  [sum_block(): return lax.psum(local_cross, 'smp')]
    reduce_sum x0 -> x2, other arithmetic: none -> 3.57 us  [gather_and_add(): total = terms.sum(axis=0)]
  transfers between devices with their start and end apart: 3 -> 4, of which waited for: 3 -> 4; matrix products, arithmetic and copies ran while one was open for 2% -> 4% of each run, Pallas kernels for 0% -> 0%
where the time goes in v1:
time: 244 us; the launch traced here: 243 us
  waiting for transfers between devices  187 us (77%)
  other arithmetic  14 us (6%)
  between operations  14 us (6%)
  blocking collectives  12.1 us (5%)
  matrix products  12 us (5%)
  local copies, waits for them, and re-layouts  3.79 us (2%)
    all_gather x2, waiting for transfers between devices, gather_and_add(): terms = lax.all_gather(x, mesh_axis, axis=0, tiled=False)  89.6 us
    reduce_scatter x1, waiting for transfers between devices, per_device(): lax.psum_scatter(lax.dot_general(stacked, old_all, contract, preferred_el...  72.1 us
    all_gather x1, waiting for transfers between devices, per_device(): gathered = lax.all_gather(joined, 'blk', axis=1, tiled=True)  25.6 us
    psum x1, blocking collectives, per_device(): lax.psum(lax.dot_general(added_columns, right_side, contract, preferred_e...  12.1 us
  transfers between devices with their start and end apart: 4, of which 4 were waited for; matrix products, arithmetic and copies ran while one was open for 4% of the time, Pallas kernels for 0%

profile of v1, /device:TPU:0, one launch (start us, length us, event | category | flops | bytes accessed | tf_op | source)
XLA Modules:
  0.0 243.4 jit_solution(12934722728782286256)
XLA Ops:
  7.2 0.7 fusion.29
  7.9 0.9 broadcast_multiply_fusion
  8.8 1.6 convolution_convert_fusion.1
  10.4 1.1 fusion.36
  11.6 1.7 convolution_convert_fusion
  13.4 1.1 fusion.37
  15.0 45.1 %all-gather.8.cloned.1.call-done = f32[2048,256]{1,0:T(8,128)} async-done(((f32[512,256]{1,0:T(8,128)}), f32[2048,256]{1,0:T(8,128)}) %all-gather.8.cloned.1.call-update) | async-done | bytes 2097168 | tf_op jit(solution)/shard_map/all_gather | solution.py:10
  60.1 1.8 reduce_sum.36
  62.2 44.5 %all-gather.10.cloned.1.call-done = f32[2048,256]{1,0:T(8,128)} async-done(((f32[512,256]{1,0:T(8,128)}), f32[2048,256]{1,0:T(8,128)}) %all-gather.10.cloned.1.call-update) | async-done | bytes 2097168 | tf_op jit(solution)/shard_map/all_gather | solution.py:10
  106.7 1.8 reduce_sum.38
  108.8 0.5 multiply_convert_fusion
  109.5 0.3 convolution_multiply_fusion.3
  110.2 0.3 fusion.2
  110.5 0.3 fusion.5
  110.9 0.3 fusion.1
  111.2 0.3 fusion.4
  111.6 0.3 fusion.7
  111.9 0.3 fusion.6
  112.3 0.9 pad_maximum_fusion
  113.3 0.7 slice.104
  114.0 25.6 %all-gather.6.cloned.1.call-done = bf16[512,1552]{0,1:T(8,128)(2,1)} async-done(((bf16[512,776]{0,1:T(8,128)(2,1)}), bf16[512,1552]{0,1:T(8,128)(2,1)}) %all-gather.6.cloned.1.call-update) | async-done | bytes 1589264 | tf_op jit(solution)/shard_map/all_gather | solution.py:95
  139.6 1.5 slice.126
  141.1 3.6 %fusion.9 = f32[777,1536]{1,0:T(8,128)} fusion(bf16[512,1536]{0,1:T(8,128)(2,1)S(1)} %bitcast.79, bf16[512,1]{0,1:T(2,128)(2,1)S(1)} %slice.104, bf16[512,8]{0,1:T(8,128)(2,1)S(1)} %reshape_squeeze.35, bf16[512,768]{0,1:T(8,128)(2,1)S(1)} %bitcast.68), kind=kOutput, calls=%fused_computation.22 | convolution fusion | flops 1224502272 | bytes 7142400 | tf_op jit(solution)/shard_map/dot_general | solution.py:102
  144.8 0.8 pad_maximum_fusion.1
  145.6 0.7 slice_bitcast_fusion
  146.4 12.1 %psum.7 = f32[8,17]{1,0:T(8,128)S(1)} all-reduce(f32[8,17]{1,0:T(8,128)S(1)} %fusion.21), channel_id=1, replica_groups=mesh['grp'=2,'smp'=4,'blk'=2,'pen'=2] {'smp'}, use_global_device_ids=true, to_apply=%region_5.0 | all-reduce | flops 136 | bytes 1088 | tf_op jit(solution)/shard_map/psum | solution.py:111
  158.5 0.7 multiply_reduce_fusion
  159.2 0.6 multiply_bitcast_fusion
  159.8 72.1 %reduce-scatter.2.cloned.1.call-done = f32[777,384]{1,0:T(8,128)} async-done(((f32[777,1536]{1,0:T(8,128)}), f32[777,384]{1,0:T(8,128)}) %reduce-scatter.2.cloned.1.call-update) | async-done | bytes 1193488 | tf_op jit(solution)/shard_map/reduce_scatter | solution.py:101
  231.9 1.3 slice_multiply_fusion.2
  233.2 1.3 fusion.27
  234.5 2.4 fusion.8
  (30 shorter events, 1.9 us)
Async XLA Ops:
  7.2 52.9 %all-gather.8.cloned.1.call-start = ((), (), s32[]{:S(2)}) async-start(), calls=%async_computation.3 | async-start | bytes 2621440 | tf_op jit(solution)/shard_map/all_gather | solution.py:10
  11.6 3.0 %copy-start = (bf16[1,512,768]{2,1,0:T(8,128)(2,1)S(1)}, bf16[1,512,768]{2,1,0:T(8,128)(2,1)}, u32[]{:S(2)}) copy-start(bf16[1,512,768]{2,1,0:T(8,128)(2,1)} %param.13) | copy-start | bytes 2359300
  11.6 95.2 %all-gather.10.cloned.1.call-start = ((), (), s32[]{:S(2)}) async-start(), calls=%async_computation.4 | async-start | bytes 2621440 | tf_op jit(solution)/shard_map/all_gather | solution.py:10
  13.3 1.5 copy-start.1
  13.3 1.6 copy-start.2
  14.5 125.1 %all-gather.6.cloned.1.call-start = ((), (), s32[]{:S(2)}) async-start(), calls=%async_computation.1 | async-start | bytes 2383872 | tf_op jit(solution)/shard_map/all_gather | solution.py:95
  113.3 118.6 %reduce-scatter.2.cloned.1.call-start = ((), (), s32[]{:S(2)}) async-start(), calls=%async_computation.2 | async-start | bytes 6021120 | tf_op jit(solution)/shard_map/reduce_scatter | solution.py:101
Sparse Core Ops, SparseCore 0:
  11.7 48.3 all-gather.7
  62.2 44.4 all-gather.9
  113.4 26.1 all-gather.5
  144.9 87.0 reduce-scatter.1

commit v2 on v0

--- a/solution.py
+++ b/solution.py
@@ -86,7 +86,7 @@
     old_width = old_cols.shape[1]
     new_width = added_columns.shape[1]
     joined = jnp.concatenate([old_cols, added_columns], axis=1)
-    gathered = lax.all_gather(joined, "blk", axis=1, tiled=True)
+    gathered = jnp.concatenate(jax.lax.all_gather(joined, axis_name="blk"), 1)
     shard_count = gathered.shape[1] // joined.shape[1]
     pieces = gathered.reshape(row_count, shard_count, joined.shape[1])
     old_all = pieces[:, :, :old_width].reshape(row_count, shard_count * old_width)

time: 205 us -> 214 us (1.044)
  local copies, waits for them, and re-layouts: 3.02 us -> 7.73 us
  waiting for transfers between devices: 153 us -> 157 us
    all_gather x0 -> x1, local copies, waits for them, and re-layouts: none -> 4.74 us  [per_device(): gathered = jnp.concatenate(jax.lax.all_gather(joined, axis_name='blk'), 1)]
    all_gather x1, waiting for transfers between devices: 26.7 us -> 29.3 us  [per_device(): gathered = jnp.concatenate(jax.lax.all_gather(joined, axis_name='blk'), 1)]
  transfers between devices with their start and end apart: 3 -> 3, of which waited for: 3 -> 3; matrix products, arithmetic and copies ran while one was open for 2% -> 1% of each run, Pallas kernels for 0% -> 0%
where the time goes in v2:
time: 214 us
  waiting for transfers between devices  157 us (73%)
  between operations  14.1 us (7%)
  matrix products  12.1 us (6%)
  blocking collectives  12 us (6%)
  other arithmetic  11.1 us (5%)
  local copies, waits for them, and re-layouts  7.73 us (4%)
    reduce_scatter x1, waiting for transfers between devices, per_device(): lax.psum_scatter(lax.dot_general(stacked, old_all, contract, preferred_el...  72.8 us
    psum x1, waiting for transfers between devices, sum_block(): return lax.psum(local_cross, 'smp')  54.6 us
    all_gather x1, waiting for transfers between devices, per_device(): gathered = jnp.concatenate(jax.lax.all_gather(joined, axis_name='blk'), 1)  29.3 us
    psum x1, blocking collectives, per_device(): lax.psum(lax.dot_general(added_columns, right_side, contract, preferred_e...  12 us
    all_gather x1, local copies, waits for them, and re-layouts, per_device(): gathered = jnp.concatenate(jax.lax.all_gather(joined, axis_name='blk'), 1)  4.74 us
  transfers between devices with their start and end apart: 3, of which 3 were waited for; matrix products, arithmetic and copies ran while one was open for 1% of the time, Pallas kernels for 0%

profile of v2, /device:TPU:0, one launch (start us, length us, event | category | flops | bytes accessed | tf_op | source)
XLA Modules:
  0.0 213.9 jit_solution(17380123293318194842)
XLA Ops:
  7.2 1.7 convolution_convert_fusion
  9.0 1.5 convolution_convert_fusion.1
  10.5 1.1 fusion.36
  11.6 1.1 fusion.37
  12.9 54.6 %all-reduce.3.cloned.1.call-done = (f32[512,4,64]{0,2,1:T(8,128)}, f32[512,4,64]{0,2,1:T(8,128)}) async-done(((f32[512,4,64]{0,2,1:T(8,128)}, f32[512,4,64]{0,2,1:T(8,128)}), (f32[512,4,64]{0,2,1:T(8,128)}, f32[512,4,64]{0,2,1:T(8,128)})) %all-reduce.3.cloned.1.call-update) | async-done | bytes 1048592 | tf_op jit(solution)/shard_map/psum | solution.py:34
  67.6 1.1 reduce_sum.19
  68.7 1.1 broadcast_subtract_fusion
  70.0 0.5 multiply_convert_fusion
  70.7 0.3 convolution_multiply_fusion.3
  71.0 0.3 convolution_multiply_fusion.7
  71.3 0.3 fusion.2
  71.7 0.3 fusion.5
  72.0 0.3 fusion.1
  72.4 0.3 fusion.4
  72.7 0.3 fusion.7
  73.1 0.3 fusion.6
  73.6 0.2 copy-done.1
  73.8 1.0 pad_maximum_fusion
  75.1 29.3 %all-gather.3.cloned.1.call-done = bf16[1024,776]{1,0:T(8,128)(2,1)} async-done(((bf16[512,776]{1,0:T(8,128)(2,1)}), bf16[1024,776]{1,0:T(8,128)(2,1)}) %all-gather.3.cloned.1.call-update) | async-done | bytes 1589264 | tf_op jit(solution)/shard_map/all_gather | solution.py:89
  104.4 4.7 %copy.28 = bf16[2,512,776]{1,0,2:T(2,128)(2,1)S(1)} copy(bf16[2,512,776]{2,1,0:T(8,128)(2,1)} %bitcast.73) | data formatting | bytes 3178496 | tf_op jit(solution)/shard_map/all_gather | solution.py:89
  109.1 1.1 slice.126
  110.2 0.3 copy.26
  110.5 0.9 copy-done.2
  111.4 3.9 %fusion.9 = f32[777,1536]{1,0:T(8,128)} fusion(bf16[512,1536]{0,1:T(8,128)(2,1)S(1)} %bitcast.74, bf16[512,1]{1,0:T(8,128)(2,1)S(1)} %copy.23, bf16[512,8]{1,0:T(8,128)(2,1)S(1)} %copy.22, bf16[512,768]{1,0:T(8,128)(2,1)S(1)} %bitcast.84), kind=kOutput, calls=%fused_computation.22 | convolution fusion | flops 1224502272 | bytes 7142400 | tf_op jit(solution)/shard_map/dot_general | solution.py:96
  115.3 0.8 pad_maximum_fusion.1
  116.3 12.0 %psum.23 = f32[8,17]{1,0:T(8,128)S(1)} all-reduce(f32[8,17]{1,0:T(8,128)S(1)} %fusion.21), channel_id=1, replica_groups=mesh['grp'=2,'smp'=4,'blk'=2,'pen'=2] {'smp'}, use_global_device_ids=true, to_apply=%region_5.0 | all-reduce | flops 136 | bytes 1088 | tf_op jit(solution)/shard_map/psum | solution.py:105
  128.3 0.7 multiply_reduce_fusion
  129.0 0.6 multiply_bitcast_fusion
  129.6 72.8 %reduce-scatter.2.cloned.1.call-done = f32[777,384]{1,0:T(8,128)} async-done(((f32[777,1536]{1,0:T(8,128)}), f32[777,384]{1,0:T(8,128)}) %reduce-scatter.2.cloned.1.call-update) | async-done | bytes 1193488 | tf_op jit(solution)/shard_map/reduce_scatter | solution.py:95
  202.4 1.3 slice_multiply_fusion.2
  203.7 1.3 fusion.27
  205.0 2.4 %fusion.8 = f32[1,768,384]{2,1,0:T(8,128)} fusion(f32[777,384]{1,0:T(8,128)} %reduce-scatter.2.cloned.1.call-done), kind=kLoop, calls=%fused_computation.21 | loop fusion | flops 294912 | bytes 2359296 | tf_op jit(solution)/shard_map/broadcast_in_dim | solution.py:113
  (37 shorter events, 1.1 us)
Async XLA Ops:
  7.2 1.8 copy-start.7
  7.2 3.3 %copy-start.5 = (s32[512]{0:T(512)S(1)}, s32[512]{0:T(512)}, u32[]{:S(2)}) copy-start(s32[512]{0:T(512)} %param.12) | copy-start | bytes 6148
  7.2 3.3 %copy-start.3 = (bf16[512,64]{0,1:T(8,128)(2,1)S(1)}, bf16[512,64]{0,1:T(8,128)(2,1)}, u32[]{:S(2)}) copy-start(bf16[512,64]{0,1:T(8,128)(2,1)} %param.11) | copy-start | bytes 196612
  7.2 60.4 %all-reduce.3.cloned.1.call-start = ((), (), s32[]{:S(2)}) async-start(), calls=%async_computation.3 | async-start | bytes 2097152 | tf_op jit(solution)/shard_map/psum | solution.py:34
  10.5 2.3 %copy-start.4 = (f32[2,512]{1,0:T(2,128)S(1)}, f32[2,512]{1,0:T(2,128)}, u32[]{:S(2)}) copy-start(f32[2,512]{1,0:T(2,128)} %param.9) | copy-start | bytes 12292
  10.5 2.3 %copy-start.6 = (f32[4]{0:T(128)S(1)}, f32[4]{0:T(128)}, u32[]{:S(2)}) copy-start(f32[4]{0:T(128)} %param.10) | copy-start | bytes 52
  12.8 91.6 %all-gather.3.cloned.1.call-start = ((), (), s32[]{:S(2)}) async-start(), calls=%async_computation.2 | async-start | bytes 2752512 | tf_op jit(solution)/shard_map/all_gather | solution.py:89
  67.6 2.3 %copy-start = (f32[512,4,64]{0,2,1:T(8,128)S(1)}, f32[512,4,64]{0,2,1:T(8,128)}, u32[]{:S(2)}) copy-start(f32[512,4,64]{0,2,1:T(8,128)} %get-tuple-element.7) | copy-start | bytes 1572868
  72.7 1.1 copy-start.1
  74.9 127.6 %reduce-scatter.2.cloned.1.call-start = ((), (), s32[]{:S(2)}) async-start(), calls=%async_computation.1 | async-start | bytes 6021120 | tf_op jit(solution)/shard_map/reduce_scatter | solution.py:95
  110.2 1.1 copy-start.2
Sparse Core Ops, SparseCore 0:
  12.9 54.6 all-reduce.2
  75.0 29.3 all-gather.2
  115.4 86.9 reduce-scatter.1
